TPU v7x, 32 devices: a whole 2x2x4 slice. The times are simulated.
32 devices in a mesh: section: 4 (over z), dp: 8 (over y, x, core).
Axes of the slice: x: 2, y: 2, z: 4, core: 2. Of those that a mesh axis runs over, the one named last changes fastest.
Arguments:
- embedded: bfloat16 [2, 1024, 4096], P(None, 'dp'), may hold values from -6 to 6
- saved_inputs: bfloat16 [4, 2, 1024, 4096], P('section', None, 'dp'), may hold values from -6 to 6
- cotangent: bfloat16 [2, 1024, 4096], P(None, 'dp'), may hold values from -6 to 6
- w_down: bfloat16 [4, 512, 4096], P('section'), may hold values from -0.09375 to 0.09375
- w_up: bfloat16 [4, 512, 4096], P('section'), may hold values from -0.046875 to 0.046875
- bias: float32 [4, 4096], P('section'), may hold values from -3 to 3
- owners: int32 [1024, 2, 16, 1], P('dp'), may hold values from 0 to 31; in each aligned block of 1024 rows (0 to 1023, 1024 to 2047, ..., all dimensions but the last counted through in order) at most 64 rows name the same one
- row_ids: int32 [1024, 2, 16], P('dp'), may hold values from 0 to 2047
Outputs:
- grad_down: float32 [4, 512, 4096], P('section', None, 'dp')
- grad_up: float32 [4, 512, 4096], P('section', None, 'dp')
- grad_bias: float32 [4, 4096], P('section', 'dp')
- table_grad: float32 [65536, 256], P(('section', 'dp'))
Inputs may be any that keep to these rules, and one draw needn't show every extreme that they name: `owners`: in each aligned block of 1024 lookups in the order (sample, micro-batch, feature) no owner is named more than 64 times, a bound that some block reaches.
All inputs are finite; a program needn't handle non-finite values.
Results may differ from a plain program's by a relative error of at most 0.015.
Values may be sent and summed in bfloat16 or wider, within the bound.
A program may use at most 192 MiB of HBM per device.

v0:
```python
import jax
import jax.numpy as jnp
from jax import lax
from jax.sharding import PartitionSpec as P

E = 256
ROWS_DEV = 2048


def from_behind(block, axis, distance):
    devices = range(lax.axis_size(axis))
    route = [(i - distance, i) for i in devices if i - distance in devices]
    return lax.ppermute(block, axis, route)


def local(embedded, saved_inputs, cotangent, w_down, w_up, bias, owners, row_ids):
    sections = lax.axis_size("section")
    replicas = lax.axis_size("dp")
    section_id = lax.axis_index("section")
    micro_count, samples, width = embedded.shape
    rank = w_down.shape[1]
    pieces_per = 1
    piece_rows = samples // pieces_per
    piece_count = micro_count * pieces_per
    turns = sections + piece_count - 1
    down_mat = w_down[0]
    up_mat = w_up[0]
    bias_row = bias[0]

    def turn(step, carry):
        incoming, accum, acc_bias, stores = carry
        piece = step - (sections - 1 - section_id)
        valid = (piece >= 0) & (piece < piece_count)
        gate = jnp.where(valid, 1.0, 0.0).astype(jnp.float32)
        clipped = jnp.clip(piece, 0, piece_count - 1)
        micro = clipped // pieces_per
        offset = clipped % pieces_per * piece_rows
        zero = jnp.int32(0)
        first = lax.dynamic_slice(embedded, (micro, offset, zero), (1, piece_rows, width))[
            0
        ].astype(jnp.float32)
        layer_in = lax.dynamic_slice(
            saved_inputs, (zero, micro, offset, zero), (1, 1, piece_rows, width)
        )[0, 0]
        top_grad = lax.dynamic_slice(cotangent, (micro, offset, zero), (1, piece_rows, width))[0]
        upstream = jnp.where(section_id == sections - 1, top_grad, incoming).astype(jnp.float32)
        latent = lax.dot_general(
            layer_in, down_mat, (((1,), (1,)), ((), ())), preferred_element_type=jnp.float32
        ).astype(jnp.bfloat16)
        product = jnp.dot(latent, up_mat, preferred_element_type=jnp.float32) + bias_row
        grad_prod = upstream * first
        grad_prod_b = grad_prod.astype(jnp.bfloat16)
        acc_bias = acc_bias + gate * jnp.sum(grad_prod, axis=0)
        grad_latent = lax.dot_general(
            grad_prod_b, up_mat, (((1,), (1,)), ((), ())), preferred_element_type=jnp.float32
        ).astype(jnp.bfloat16)
        acc_up, acc_down = stores
        acc_up = acc_up + gate * lax.dot_general(
            latent, grad_prod_b, (((0,), (0,)), ((), ())), preferred_element_type=jnp.float32
        )
        acc_down = acc_down + gate * lax.dot_general(
            grad_latent, layer_in, (((0,), (0,)), ((), ())), preferred_element_type=jnp.float32
        )
        stores = (acc_up, acc_down)
        passed = upstream + jnp.dot(grad_latent, down_mat, preferred_element_type=jnp.float32)
        term = upstream * product + jnp.where(section_id == 0, passed, 0.0)
        current = lax.dynamic_slice(accum, (micro, offset, zero), (1, piece_rows, width))
        accum = lax.dynamic_update_slice(accum, current + gate * term[None], (micro, offset, zero))
        sent = from_behind(passed.astype(jnp.bfloat16), "section", -1)
        return (sent, accum, acc_bias, stores)

    stores = (jnp.zeros((rank, width), jnp.float32), jnp.zeros((rank, width), jnp.float32))
    start = (
        jnp.zeros((piece_rows, width), jnp.bfloat16),
        jnp.zeros((micro_count, samples, width), jnp.float32),
        jnp.zeros((width,), jnp.float32),
        stores,
    )
    final = lax.fori_loop(0, turns, turn, start)
    accum, acc_bias, stores = (final[1], final[2], final[3])
    acc_up, acc_down = stores
    stacked = jnp.concatenate([acc_down, acc_up, acc_bias[None]], axis=0)[None]
    reduced = lax.psum_scatter(stacked, "dp", scatter_dimension=2, tiled=True)
    grad_down = reduced[:, :rank]
    grad_up = reduced[:, rank : 2 * rank]
    grad_bias = reduced[:, 2 * rank]
    shared = lax.psum_scatter(
        accum.astype(jnp.bfloat16), "section", scatter_dimension=1, tiled=True
    ).astype(jnp.float32)
    sub_rows = shared.shape[1]
    features = width // E
    row_grads = (
        shared.reshape(micro_count, sub_rows, features, E).transpose(1, 0, 2, 3).reshape(-1, E)
    )
    own_slice = lax.dynamic_slice_in_dim(owners, section_id * sub_rows, sub_rows, 0).reshape(-1)
    id_slice = lax.dynamic_slice_in_dim(row_ids, section_id * sub_rows, sub_rows, 0).reshape(-1)
    look = own_slice.shape[0]
    devices = sections * replicas
    capacity = max(2, (2 * look + devices - 1) // devices)
    targets = (own_slice[:, None] == jnp.arange(devices, dtype=jnp.int32)[None, :]).astype(
        jnp.int32
    )
    slot_of = jnp.sum((jnp.cumsum(targets, axis=0) - 1) * targets, axis=1)
    send_vals = jnp.zeros((devices, capacity, E), jnp.float32).at[own_slice, slot_of].set(row_grads)
    send_rows = jnp.zeros((devices, capacity), jnp.int32).at[own_slice, slot_of].set(id_slice)
    got_vals, got_rows = (
        lax.all_to_all(
            send_vals.astype(jnp.bfloat16),
            ("section", "dp"),
            split_axis=0,
            concat_axis=0,
            tiled=True,
        ).astype(send_vals.dtype),
        lax.all_to_all(send_rows, ("section", "dp"), split_axis=0, concat_axis=0, tiled=True),
    )
    table_grad = jax.ops.segment_sum(
        got_vals.reshape(-1, E), got_rows.reshape(-1), num_segments=ROWS_DEV
    )
    return (grad_down, grad_up, grad_bias, table_grad)


def solution(mesh):
    placed = (
        P(None, "dp", None),
        P("section", None, "dp", None),
        P(None, "dp", None),
        P("section", None, None),
        P("section", None, None),
        P("section", None),
        P("dp", None, None, None),
        P("dp", None, None),
    )
    return jax.shard_map(
        local,
        mesh=mesh,
        in_specs=placed,
        out_specs=(
            P("section", None, "dp"),
            P("section", None, "dp"),
            P("section", "dp"),
            P(("section", "dp"), None),
        ),
        check_vma=False,
    )
```

profile of v0, /device:TPU:0, one launch (start us, length us, event | category | flops | bytes accessed | tf_op | source)
XLA Modules:
  0.0 362.8 jit_solution(10234618040520422243)
XLA Ops:
  7.3 1.1 broadcast_in_dim.43
  8.3 2.4 broadcast_in_dim.44
  10.8 169.2 %while.24 = (s32[]{:T(128)}, bf16[128,4096]{1,0:T(8,128)(2,1)}, f32[2,128,4096]{2,1,0:T(8,128)}, f32[4096]{0:T(1024)S(1)}, f32[512,4096]{1,0:T(8,128)}, /*index=...) while((s32[]{:T(128)}, bf16[128,4096]{1,0:T(8,128)(2,1)}, ...), condition=%wide.region_2.3_spmd.clone, body=%wide.region_0.2_spmd.clone.sunk | while | flops 3246006272 | bytes 136135632 | solution.py:79
  10.8 2.2 fusion.65
  13.6 1.5 convolution_convert_fusion.4
  15.1 0.7 copy-done.3
  15.8 1.7 fusion.66
  17.5 1.3 collective-permute-start
  18.8 4.0 %convolution_convert_fusion.5 = bf16[128,512]{1,0:T(8,128)(2,1)S(1)} fusion(bf16[512,4096]{1,0:T(8,128)(2,1)} %get-tuple-element.569, bf16[1,2,128,4096]{3,2,1,0:T(8,128)(2,1)} %get-tuple-element.570, s32[]{:T(128)S(6)} %min.13), kind=kOutput, calls=%fused_computation.16.clone.1 | convolution fusion | flops 536936448 | bytes 5373956 | tf_op jit(solution)/shard_map/while/body/eval_jaxpr/dot_general | solution.py:47
  22.9 5.9 %select_add_fusion.8 = f32[512,4096]{1,0:T(8,128)} fusion(f32[512,4096]{1,0:T(8,128)} %get-tuple-element.543, bf16[128,512]{1,0:T(8,128)(2,1)S(1)} %convolution_convert_fusion.4, f32[]{:T(128)S(6)} %select_n.139, pred[]{:T(512)S(6)} %compare.11, bf16[1,2,128,4096]{3,2,1,0:T(8,128)(2,1)} %get-tuple-element.570, s32[]{:T(128)S(6)} %min.13), kind=kOutput, calls=%fused_computation.3.clone.1 | convolution fusion | flops 543162368 | bytes 17956872 | tf_op jit(solution)/shard_map/while/body/eval_jaxpr/dot_general | solution.py:61
  28.7 4.2 %fusion.67 = f32[2,128,4096]{2,1,0:T(8,128)} fusion(f32[2,128,4096]{2,1,0:T(8,128)} %get-tuple-element.540, s32[]{:T(128)S(6)} %min.13, bf16[128,512]{1,0:T(8,128)(2,1)S(1)} %convolution_convert_fusion.5, bf16[512,4096]{1,0:T(8,128)(2,1)S(1)} %copy-done.2, bf16[128,4096]{1,0:T(8,128)(2,1)S(1)} %get-tuple-element.514, ...), kind=kOutput, calls=%fused_computation.12.clone.1 | convolution fusion | flops 540540928 | bytes 11682312 | tf_op jit(solution)/shard_map/while/body/eval_jaxpr/dot_general | solution.py:50
  32.9 5.9 %select_add_fusion.7 = f32[512,4096]{1,0:T(8,128)} fusion(f32[512,4096]{1,0:T(8,128)} %get-tuple-element.542, bf16[128,512]{1,0:T(8,128)(2,1)S(1)} %convolution_convert_fusion.5, f32[]{:T(128)S(6)} %select_n.139, pred[]{:T(512)S(6)} %compare.11, bf16[128,4096]{1,0:T(8,128)(2,1)S(1)} %get-tuple-element.514, ...), kind=kOutput, calls=%fused_computation.4.clone.1 | convolution fusion | flops 545259520 | bytes 19005448 | tf_op jit(solution)/shard_map/while/body/eval_jaxpr/dot_general | solution.py:58
  38.8 7.1 %collective-permute-done = bf16[128,4096]{1,0:T(8,128)(2,1)} collective-permute-done((bf16[128,4096]{1,0:T(8,128)(2,1)}, bf16[128,4096]{1,0:T(8,128)(2,1)}, u32[]{:S(2)}, u32[]{:S(2)}) %collective-permute-start) | collective-permute-done | bytes 1048608 | tf_op jit(solution)/shard_map/while/body/eval_jaxpr/ppermute | solution.py:13
  45.9 2.2 fusion.65
  48.7 1.5 convolution_convert_fusion.4
  50.9 1.7 fusion.66
  52.6 1.3 collective-permute-start
  53.9 4.0 %convolution_convert_fusion.5 = bf16[128,512]{1,0:T(8,128)(2,1)S(1)} fusion(bf16[512,4096]{1,0:T(8,128)(2,1)} %get-tuple-element.569, bf16[1,2,128,4096]{3,2,1,0:T(8,128)(2,1)} %get-tuple-element.570, s32[]{:T(128)S(6)} %min.13), kind=kOutput, calls=%fused_computation.16.clone.1 | convolution fusion | flops 536936448 | bytes 5373956 | tf_op jit(solution)/shard_map/while/body/eval_jaxpr/dot_general | solution.py:47
  58.0 8.4 %select_add_fusion.8 = f32[512,4096]{1,0:T(8,128)} fusion(f32[512,4096]{1,0:T(8,128)} %get-tuple-element.543, bf16[128,512]{1,0:T(8,128)(2,1)S(1)} %convolution_convert_fusion.4, f32[]{:T(128)S(6)} %select_n.139, pred[]{:T(512)S(6)} %compare.11, bf16[1,2,128,4096]{3,2,1,0:T(8,128)(2,1)} %get-tuple-element.570, s32[]{:T(128)S(6)} %min.13), kind=kOutput, calls=%fused_computation.3.clone.1 | convolution fusion | flops 543162368 | bytes 17956872 | tf_op jit(solution)/shard_map/while/body/eval_jaxpr/dot_general | solution.py:61
  66.4 4.2 %fusion.67 = f32[2,128,4096]{2,1,0:T(8,128)} fusion(f32[2,128,4096]{2,1,0:T(8,128)} %get-tuple-element.540, s32[]{:T(128)S(6)} %min.13, bf16[128,512]{1,0:T(8,128)(2,1)S(1)} %convolution_convert_fusion.5, bf16[512,4096]{1,0:T(8,128)(2,1)S(1)} %copy-done.2, bf16[128,4096]{1,0:T(8,128)(2,1)S(1)} %get-tuple-element.514, ...), kind=kOutput, calls=%fused_computation.12.clone.1 | convolution fusion | flops 540540928 | bytes 11682312 | tf_op jit(solution)/shard_map/while/body/eval_jaxpr/dot_general | solution.py:50
  70.5 8.4 %select_add_fusion.7 = f32[512,4096]{1,0:T(8,128)} fusion(f32[512,4096]{1,0:T(8,128)} %get-tuple-element.542, bf16[128,512]{1,0:T(8,128)(2,1)S(1)} %convolution_convert_fusion.5, f32[]{:T(128)S(6)} %select_n.139, pred[]{:T(512)S(6)} %compare.11, bf16[128,4096]{1,0:T(8,128)(2,1)S(1)} %get-tuple-element.514, ...), kind=kOutput, calls=%fused_computation.4.clone.1 | convolution fusion | flops 545259520 | bytes 19005448 | tf_op jit(solution)/shard_map/while/body/eval_jaxpr/dot_general | solution.py:58
  79.1 2.2 fusion.65
  82.0 1.5 convolution_convert_fusion.4
  84.1 1.7 fusion.66
  85.8 1.3 collective-permute-start
  87.1 4.0 %convolution_convert_fusion.5 = bf16[128,512]{1,0:T(8,128)(2,1)S(1)} fusion(bf16[512,4096]{1,0:T(8,128)(2,1)} %get-tuple-element.569, bf16[1,2,128,4096]{3,2,1,0:T(8,128)(2,1)} %get-tuple-element.570, s32[]{:T(128)S(6)} %min.13), kind=kOutput, calls=%fused_computation.16.clone.1 | convolution fusion | flops 536936448 | bytes 5373956 | tf_op jit(solution)/shard_map/while/body/eval_jaxpr/dot_general | solution.py:47
  91.2 8.4 %select_add_fusion.8 = f32[512,4096]{1,0:T(8,128)} fusion(f32[512,4096]{1,0:T(8,128)} %get-tuple-element.543, bf16[128,512]{1,0:T(8,128)(2,1)S(1)} %convolution_convert_fusion.4, f32[]{:T(128)S(6)} %select_n.139, pred[]{:T(512)S(6)} %compare.11, bf16[1,2,128,4096]{3,2,1,0:T(8,128)(2,1)} %get-tuple-element.570, s32[]{:T(128)S(6)} %min.13), kind=kOutput, calls=%fused_computation.3.clone.1 | convolution fusion | flops 543162368 | bytes 17956872 | tf_op jit(solution)/shard_map/while/body/eval_jaxpr/dot_general | solution.py:61
  99.6 4.2 %fusion.67 = f32[2,128,4096]{2,1,0:T(8,128)} fusion(f32[2,128,4096]{2,1,0:T(8,128)} %get-tuple-element.540, s32[]{:T(128)S(6)} %min.13, bf16[128,512]{1,0:T(8,128)(2,1)S(1)} %convolution_convert_fusion.5, bf16[512,4096]{1,0:T(8,128)(2,1)S(1)} %copy-done.2, bf16[128,4096]{1,0:T(8,128)(2,1)S(1)} %get-tuple-element.514, ...), kind=kOutput, calls=%fused_computation.12.clone.1 | convolution fusion | flops 540540928 | bytes 11682312 | tf_op jit(solution)/shard_map/while/body/eval_jaxpr/dot_general | solution.py:50
  103.7 8.4 %select_add_fusion.7 = f32[512,4096]{1,0:T(8,128)} fusion(f32[512,4096]{1,0:T(8,128)} %get-tuple-element.542, bf16[128,512]{1,0:T(8,128)(2,1)S(1)} %convolution_convert_fusion.5, f32[]{:T(128)S(6)} %select_n.139, pred[]{:T(512)S(6)} %compare.11, bf16[128,4096]{1,0:T(8,128)(2,1)S(1)} %get-tuple-element.514, ...), kind=kOutput, calls=%fused_computation.4.clone.1 | convolution fusion | flops 545259520 | bytes 19005448 | tf_op jit(solution)/shard_map/while/body/eval_jaxpr/dot_general | solution.py:58
  112.8 2.2 fusion.65
  115.6 1.5 convolution_convert_fusion.4
  117.1 0.7 copy-done.3
  117.8 1.7 fusion.66
  119.5 1.3 collective-permute-start
  120.8 4.0 %convolution_convert_fusion.5 = bf16[128,512]{1,0:T(8,128)(2,1)S(1)} fusion(bf16[512,4096]{1,0:T(8,128)(2,1)} %get-tuple-element.569, bf16[1,2,128,4096]{3,2,1,0:T(8,128)(2,1)} %get-tuple-element.570, s32[]{:T(128)S(6)} %min.13), kind=kOutput, calls=%fused_computation.16.clone.1 | convolution fusion | flops 536936448 | bytes 5373956 | tf_op jit(solution)/shard_map/while/body/eval_jaxpr/dot_general | solution.py:47
  124.9 8.4 %select_add_fusion.8 = f32[512,4096]{1,0:T(8,128)} fusion(f32[512,4096]{1,0:T(8,128)} %get-tuple-element.543, bf16[128,512]{1,0:T(8,128)(2,1)S(1)} %convolution_convert_fusion.4, f32[]{:T(128)S(6)} %select_n.139, pred[]{:T(512)S(6)} %compare.11, bf16[1,2,128,4096]{3,2,1,0:T(8,128)(2,1)} %get-tuple-element.570, s32[]{:T(128)S(6)} %min.13), kind=kOutput, calls=%fused_computation.3.clone.1 | convolution fusion | flops 543162368 | bytes 17956872 | tf_op jit(solution)/shard_map/while/body/eval_jaxpr/dot_general | solution.py:61
  133.2 4.2 %fusion.67 = f32[2,128,4096]{2,1,0:T(8,128)} fusion(f32[2,128,4096]{2,1,0:T(8,128)} %get-tuple-element.540, s32[]{:T(128)S(6)} %min.13, bf16[128,512]{1,0:T(8,128)(2,1)S(1)} %convolution_convert_fusion.5, bf16[512,4096]{1,0:T(8,128)(2,1)S(1)} %copy-done.2, bf16[128,4096]{1,0:T(8,128)(2,1)S(1)} %get-tuple-element.514, ...), kind=kOutput, calls=%fused_computation.12.clone.1 | convolution fusion | flops 540540928 | bytes 11682312 | tf_op jit(solution)/shard_map/while/body/eval_jaxpr/dot_general | solution.py:50
  137.4 8.4 %select_add_fusion.7 = f32[512,4096]{1,0:T(8,128)} fusion(f32[512,4096]{1,0:T(8,128)} %get-tuple-element.542, bf16[128,512]{1,0:T(8,128)(2,1)S(1)} %convolution_convert_fusion.5, f32[]{:T(128)S(6)} %select_n.139, pred[]{:T(512)S(6)} %compare.11, bf16[128,4096]{1,0:T(8,128)(2,1)S(1)} %get-tuple-element.514, ...), kind=kOutput, calls=%fused_computation.4.clone.1 | convolution fusion | flops 545259520 | bytes 19005448 | tf_op jit(solution)/shard_map/while/body/eval_jaxpr/dot_general | solution.py:58
  146.4 2.2 fusion.65
  149.2 1.5 convolution_convert_fusion.4
  150.8 0.7 copy-done.3
  151.4 1.7 fusion.66
  153.1 1.3 collective-permute-start
  154.4 4.0 %convolution_convert_fusion.5 = bf16[128,512]{1,0:T(8,128)(2,1)S(1)} fusion(bf16[512,4096]{1,0:T(8,128)(2,1)} %get-tuple-element.569, bf16[1,2,128,4096]{3,2,1,0:T(8,128)(2,1)} %get-tuple-element.570, s32[]{:T(128)S(6)} %min.13), kind=kOutput, calls=%fused_computation.16.clone.1 | convolution fusion | flops 536936448 | bytes 5373956 | tf_op jit(solution)/shard_map/while/body/eval_jaxpr/dot_general | solution.py:47
  158.5 8.4 %select_add_fusion.8 = f32[512,4096]{1,0:T(8,128)} fusion(f32[512,4096]{1,0:T(8,128)} %get-tuple-element.543, bf16[128,512]{1,0:T(8,128)(2,1)S(1)} %convolution_convert_fusion.4, f32[]{:T(128)S(6)} %select_n.139, pred[]{:T(512)S(6)} %compare.11, bf16[1,2,128,4096]{3,2,1,0:T(8,128)(2,1)} %get-tuple-element.570, s32[]{:T(128)S(6)} %min.13), kind=kOutput, calls=%fused_computation.3.clone.1 | convolution fusion | flops 543162368 | bytes 17956872 | tf_op jit(solution)/shard_map/while/body/eval_jaxpr/dot_general | solution.py:61
  166.9 4.1 %fusion.67 = f32[2,128,4096]{2,1,0:T(8,128)} fusion(f32[2,128,4096]{2,1,0:T(8,128)} %get-tuple-element.540, s32[]{:T(128)S(6)} %min.13, bf16[128,512]{1,0:T(8,128)(2,1)S(1)} %convolution_convert_fusion.5, bf16[512,4096]{1,0:T(8,128)(2,1)S(1)} %copy-done.2, bf16[128,4096]{1,0:T(8,128)(2,1)S(1)} %get-tuple-element.514, ...), kind=kOutput, calls=%fused_computation.12.clone.1 | convolution fusion | flops 540540928 | bytes 11682312 | tf_op jit(solution)/shard_map/while/body/eval_jaxpr/dot_general | solution.py:50
  171.0 8.4 %select_add_fusion.7 = f32[512,4096]{1,0:T(8,128)} fusion(f32[512,4096]{1,0:T(8,128)} %get-tuple-element.542, bf16[128,512]{1,0:T(8,128)(2,1)S(1)} %convolution_convert_fusion.5, f32[]{:T(128)S(6)} %select_n.139, pred[]{:T(512)S(6)} %compare.11, bf16[128,4096]{1,0:T(8,128)(2,1)S(1)} %get-tuple-element.514, ...), kind=kOutput, calls=%fused_computation.4.clone.1 | convolution fusion | flops 545259520 | bytes 19005448 | tf_op jit(solution)/shard_map/while/body/eval_jaxpr/dot_general | solution.py:58
  180.0 3.8 %convert_element_type.77 = bf16[2,128,4096]{2,1,0:T(8,128)(2,1)} convert(f32[2,128,4096]{2,1,0:T(8,128)} %get-tuple-element.582) | non-fusion elementwise | flops 1048576 | bytes 6291456 | tf_op jit(solution)/shard_map/convert_element_type | solution.py:88
  183.9 12.0 %maximum_bitcast_fusion = f32[1,1025,4096]{2,1,0:T(8,128)} fusion(f32[1,4096]{1,0:T(1,128)S(1)} %bitcast.105, f32[512,4096]{1,0:T(8,128)} %get-tuple-element.584, f32[512,4096]{1,0:T(8,128)} %get-tuple-element.585), kind=kLoop, calls=%fused_computation.28 | loop fusion | flops 8396800 | bytes 33587200 | tf_op jit(solution)/shard_map/broadcast_in_dim | solution.py:82
  196.4 9.0 %reduce-window.6 = s32[32,8,128]{2,1,0:T(8,128)S(1)} reduce-window(s32[32,8,128]{2,1,0:T(8,128)S(1)} %fusion.25, s32[]{:T(128)} %constant.129.clone.1), window={size=1x1x128 pad=0_0x0_0x127_0}, to_apply=%region_4.5 | reduce-window | flops 4161536 | bytes 262148 | tf_op jit(solution)/shard_map/reduce-window
  206.4 4.3 %scatter_custom_fusion.1 = s32[2048]{0:T(1024)S(1)} fusion(s32[1024]{0:T(1024)S(1)} %broadcast_select_fusion, s32[1024]{0:T(1024)S(1)} %reshape.137, s32[]{:T(128)} %constant.129.clone.1), kind=kCustom, calls=%fused_computation.47 | custom fusion | bytes 8196
  210.8 0.7 all_to_all.9
  211.4 8.8 %all-to-all-start = ((s32[32,1,64]{2,1,0:T(1,128)}), s32[32,1,64]{2,1,0:T(1,128)S(1)}, u32[]{:S(2)}, u32[]{:S(2)}) async-start(s32[32,1,64]{2,1,0:T(1,128)} %all_to_all.9), calls=%async_computation.1 | async-start | bytes 32768 | tf_op jit(solution)/shard_map/all_to_all | solution.py:114
  220.3 11.6 %reduce-scatter.5.cloned.1.call-done = bf16[2,32,4096]{2,1,0:T(8,128)(2,1)} async-done(((bf16[2,128,4096]{2,1,0:T(8,128)(2,1)}), bf16[2,32,4096]{2,1,0:T(8,128)(2,1)}) %reduce-scatter.5.cloned.1.call-update) | async-done | bytes 524304 | tf_op jit(solution)/shard_map/reduce_scatter | solution.py:87
  231.9 1.2 copy.21
  233.2 5.3 %scatter_custom_fusion.2 = f32[2048,256]{1,0:T(8,128)S(1)} fusion(s32[1024]{0:T(1024)S(1)} %broadcast_select_fusion, f32[1024,256]{1,0:T(8,128)S(1)} %bitcast.104, f32[]{:T(128)} %constant.131.clone.1), kind=kCustom, calls=%fused_computation.32 | custom fusion | bytes 2097156
  238.5 1.1 convert_element_type.80
  239.6 3.8 %all-to-all-start.1 = ((bf16[32,64,256]{2,1,0:T(8,128)(2,1)}), bf16[32,64,256]{2,1,0:T(8,128)(2,1)S(1)}, u32[]{:S(2)}, u32[]{:S(2)}) async-start(bf16[32,64,256]{2,1,0:T(8,128)(2,1)} %bitcast.10), calls=%async_computation.3 | async-start | bytes 2097152 | tf_op jit(solution)/shard_map/all_to_all | solution.py:107
  243.9 0.7 reduce.9
  244.7 24.9 %all-to-all-done.1 = bf16[32,64,256]{2,1,0:T(8,128)(2,1)S(1)} async-done(((bf16[32,64,256]{2,1,0:T(8,128)(2,1)}), bf16[32,64,256]{2,1,0:T(8,128)(2,1)S(1)}, u32[]{:S(2)}, u32[]{:S(2)}) %all-to-all-start.1) | async-done | bytes 1048608 | tf_op jit(solution)/shard_map/all_to_all | solution.py:107
  269.6 14.8 %scatter_custom_fusion = f32[2048,256]{1,0:T(8,128)} fusion(s32[2048]{0:T(1024)S(1)} %reshape.129, bf16[2048,256]{1,0:T(8,128)(2,1)S(1)} %bitcast.102, f32[]{:T(128)} %constant.131.clone.1), kind=kCustom, calls=%fused_computation.29 | custom fusion | flops 1048576 | bytes 3145732 | tf_op jit(solution)/shard_map/scatter-add | solution.py:116
  284.4 67.3 %reduce-scatter.3.cloned.1.call-done = f32[1,1025,512]{2,1,0:T(8,128)} async-done(((f32[1,1025,4096]{2,1,0:T(8,128)}), f32[1,1025,512]{2,1,0:T(8,128)}) %reduce-scatter.3.cloned.1.call-update) | async-done | bytes 2099216 | tf_op jit(solution)/shard_map/reduce_scatter | solution.py:83
  351.7 3.0 fusion.29
  354.7 1.3 slice_bitcast_fusion
  (90 shorter events, 8.9 us)
Async XLA Ops:
  7.2 188.7 %copy-start = (s32[128,2,16,1]{0,3,2,1:T(1,128)S(1)}, s32[128,2,16,1]{0,3,2,1:T(1,128)}, u32[]{:S(2)}) copy-start(s32[128,2,16,1]{0,3,2,1:T(1,128)} %param.16) | copy-start | bytes 49156
  7.2 224.7 %reduce-scatter.5.cloned.1.call-start = ((), (), s32[]{:S(2)}) async-start(), calls=%async_computation.5 | async-start | bytes 2621440 | tf_op jit(solution)/shard_map/reduce_scatter | solution.py:87
  8.3 2.4 copy-start.4
  8.3 2.4 copy-start.6
  10.8 2.8 copy-start.1
  13.6 2.2 copy-start.3
  17.5 28.4 %collective-permute-start = (bf16[128,4096]{1,0:T(8,128)(2,1)}, bf16[128,4096]{1,0:T(8,128)(2,1)}, u32[]{:S(2)}, u32[]{:S(2)}) collective-permute-start(bf16[128,4096]{1,0:T(8,128)(2,1)} %get-tuple-element.515), channel_id=1, source_target_pairs={{8,0},{16,8},{24,16},{9,1},{17,9},{25,17},{10,2},{18,10},{26,18},{... | collective-permute-start | bytes 3145736 | tf_op jit(solution)/shard_map/while/body/eval_jaxpr/ppermute | solution.py:13
  22.8 5.9 %copy-start.2 = (bf16[512,4096]{1,0:T(8,128)(2,1)S(1)}, bf16[512,4096]{1,0:T(8,128)(2,1)}, u32[]{:S(2)}) copy-start(bf16[512,4096]{1,0:T(8,128)(2,1)} %get-tuple-element.568) | copy-start | bytes 12582916 | tf_op jit(solution)/shard_map/while
  32.9 13.0 %copy-start.5 = (bf16[2,128,4096]{2,1,0:T(8,128)(2,1)S(1)}, bf16[2,128,4096]{2,1,0:T(8,128)(2,1)}, u32[]{:S(2)}) copy-start(bf16[2,128,4096]{2,1,0:T(8,128)(2,1)} %get-tuple-element.600) | copy-start | bytes 6291460 | tf_op jit(solution)/shard_map/while
  45.9 2.8 copy-start.1
  48.7 2.2 copy-start.3
  52.6 26.5 %collective-permute-start = (bf16[128,4096]{1,0:T(8,128)(2,1)}, bf16[128,4096]{1,0:T(8,128)(2,1)}, u32[]{:S(2)}, u32[]{:S(2)}) collective-permute-start(bf16[128,4096]{1,0:T(8,128)(2,1)} %get-tuple-element.515), channel_id=1, source_target_pairs={{8,0},{16,8},{24,16},{9,1},{17,9},{25,17},{10,2},{18,10},{26,18},{... | collective-permute-start | bytes 3145736 | tf_op jit(solution)/shard_map/while/body/eval_jaxpr/ppermute | solution.py:13
  58.0 8.4 %copy-start.2 = (bf16[512,4096]{1,0:T(8,128)(2,1)S(1)}, bf16[512,4096]{1,0:T(8,128)(2,1)}, u32[]{:S(2)}) copy-start(bf16[512,4096]{1,0:T(8,128)(2,1)} %get-tuple-element.568) | copy-start | bytes 12582916 | tf_op jit(solution)/shard_map/while
  70.5 8.6 %copy-start.5 = (bf16[2,128,4096]{2,1,0:T(8,128)(2,1)S(1)}, bf16[2,128,4096]{2,1,0:T(8,128)(2,1)}, u32[]{:S(2)}) copy-start(bf16[2,128,4096]{2,1,0:T(8,128)(2,1)} %get-tuple-element.600) | copy-start | bytes 6291460 | tf_op jit(solution)/shard_map/while
  79.1 2.8 copy-start.1
  82.0 2.2 copy-start.3
  85.8 26.9 %collective-permute-start = (bf16[128,4096]{1,0:T(8,128)(2,1)}, bf16[128,4096]{1,0:T(8,128)(2,1)}, u32[]{:S(2)}, u32[]{:S(2)}) collective-permute-start(bf16[128,4096]{1,0:T(8,128)(2,1)} %get-tuple-element.515), channel_id=1, source_target_pairs={{8,0},{16,8},{24,16},{9,1},{17,9},{25,17},{10,2},{18,10},{26,18},{... | collective-permute-start | bytes 3145736 | tf_op jit(solution)/shard_map/while/body/eval_jaxpr/ppermute | solution.py:13
  91.2 8.4 %copy-start.2 = (bf16[512,4096]{1,0:T(8,128)(2,1)S(1)}, bf16[512,4096]{1,0:T(8,128)(2,1)}, u32[]{:S(2)}) copy-start(bf16[512,4096]{1,0:T(8,128)(2,1)} %get-tuple-element.568) | copy-start | bytes 12582916 | tf_op jit(solution)/shard_map/while
  103.7 9.0 %copy-start.5 = (bf16[2,128,4096]{2,1,0:T(8,128)(2,1)S(1)}, bf16[2,128,4096]{2,1,0:T(8,128)(2,1)}, u32[]{:S(2)}) copy-start(bf16[2,128,4096]{2,1,0:T(8,128)(2,1)} %get-tuple-element.600) | copy-start | bytes 6291460 | tf_op jit(solution)/shard_map/while
  112.8 2.8 copy-start.1
  115.6 2.2 copy-start.3
  119.5 26.9 %collective-permute-start = (bf16[128,4096]{1,0:T(8,128)(2,1)}, bf16[128,4096]{1,0:T(8,128)(2,1)}, u32[]{:S(2)}, u32[]{:S(2)}) collective-permute-start(bf16[128,4096]{1,0:T(8,128)(2,1)} %get-tuple-element.515), channel_id=1, source_target_pairs={{8,0},{16,8},{24,16},{9,1},{17,9},{25,17},{10,2},{18,10},{26,18},{... | collective-permute-start | bytes 3145736 | tf_op jit(solution)/shard_map/while/body/eval_jaxpr/ppermute | solution.py:13
  124.8 8.4 %copy-start.2 = (bf16[512,4096]{1,0:T(8,128)(2,1)S(1)}, bf16[512,4096]{1,0:T(8,128)(2,1)}, u32[]{:S(2)}) copy-start(bf16[512,4096]{1,0:T(8,128)(2,1)} %get-tuple-element.568) | copy-start | bytes 12582916 | tf_op jit(solution)/shard_map/while
  137.4 9.0 %copy-start.5 = (bf16[2,128,4096]{2,1,0:T(8,128)(2,1)S(1)}, bf16[2,128,4096]{2,1,0:T(8,128)(2,1)}, u32[]{:S(2)}) copy-start(bf16[2,128,4096]{2,1,0:T(8,128)(2,1)} %get-tuple-element.600) | copy-start | bytes 6291460 | tf_op jit(solution)/shard_map/while
  146.4 2.8 copy-start.1
  149.2 2.2 copy-start.3
  153.1 26.9 %collective-permute-start = (bf16[128,4096]{1,0:T(8,128)(2,1)}, bf16[128,4096]{1,0:T(8,128)(2,1)}, u32[]{:S(2)}, u32[]{:S(2)}) collective-permute-start(bf16[128,4096]{1,0:T(8,128)(2,1)} %get-tuple-element.515), channel_id=1, source_target_pairs={{8,0},{16,8},{24,16},{9,1},{17,9},{25,17},{10,2},{18,10},{26,18},{... | collective-permute-start | bytes 3145736 | tf_op jit(solution)/shard_map/while/body/eval_jaxpr/ppermute | solution.py:13
  158.5 8.4 %copy-start.2 = (bf16[512,4096]{1,0:T(8,128)(2,1)S(1)}, bf16[512,4096]{1,0:T(8,128)(2,1)}, u32[]{:S(2)}) copy-start(bf16[512,4096]{1,0:T(8,128)(2,1)} %get-tuple-element.568) | copy-start | bytes 12582916 | tf_op jit(solution)/shard_map/while
  171.0 9.0 %copy-start.5 = (bf16[2,128,4096]{2,1,0:T(8,128)(2,1)S(1)}, bf16[2,128,4096]{2,1,0:T(8,128)(2,1)}, u32[]{:S(2)}) copy-start(bf16[2,128,4096]{2,1,0:T(8,128)(2,1)} %get-tuple-element.600) | copy-start | bytes 6291460 | tf_op jit(solution)/shard_map/while
  183.8 167.9 %reduce-scatter.3.cloned.1.call-start = ((), (), s32[]{:S(2)}) async-start(), calls=%async_computation.4 | async-start | bytes 19021824 | tf_op jit(solution)/shard_map/reduce_scatter | solution.py:83
  195.9 9.9 %copy-start.7 = (s32[128,2,16]{0,2,1:T(8,128)S(1)}, s32[128,2,16]{0,2,1:T(8,128)}, u32[]{:S(2)}) copy-start(s32[128,2,16]{0,2,1:T(8,128)} %param.17) | copy-start | bytes 49156
  195.9 10.4 %copy-start.9 = (s32[2]{0:T(128)S(1)}, s32[2]{0:T(128)}, u32[]{:S(2)}) copy-start(s32[2]{0:T(128)} %constant.142) | copy-start | bytes 28
  195.9 10.5 %copy-start.8 = (s32[2]{0:T(128)S(1)}, s32[2]{0:T(128)}, u32[]{:S(2)}) copy-start(s32[2]{0:T(128)} %constant.145) | copy-start | bytes 28
  211.4 28.2 %all-to-all-start = ((s32[32,1,64]{2,1,0:T(1,128)}), s32[32,1,64]{2,1,0:T(1,128)S(1)}, u32[]{:S(2)}, u32[]{:S(2)}) async-start(s32[32,1,64]{2,1,0:T(1,128)} %all_to_all.9), calls=%async_computation.1 | async-start | bytes 32768 | tf_op jit(solution)/shard_map/all_to_all | solution.py:114
  239.6 30.0 %all-to-all-start.1 = ((bf16[32,64,256]{2,1,0:T(8,128)(2,1)}), bf16[32,64,256]{2,1,0:T(8,128)(2,1)S(1)}, u32[]{:S(2)}, u32[]{:S(2)}) async-start(bf16[32,64,256]{2,1,0:T(8,128)(2,1)} %bitcast.10), calls=%async_computation.3 | async-start | bytes 2097152 | tf_op jit(solution)/shard_map/all_to_all | solution.py:107
Sparse Core Ops, SparseCore 0:
  183.9 47.8 reduce-scatter.4
  235.5 116.1 reduce-scatter.2
where the time goes:
time: 364 us; the launch traced here: 363 us
  matrix products  136 us (37%)
  waiting for transfers between devices  113 us (31%)
  other arithmetic  52.8 us (15%)
  local copies, waits for them, and re-layouts  27.4 us (8%)
  starting transfers between devices  19.1 us (5%)
  between operations  14.2 us (4%)
    reduce_scatter x1, waiting for transfers between devices, local(): reduced = lax.psum_scatter(stacked, 'dp', scatter_dimension=2, tiled=True)  67.3 us
    dot_general x5, matrix products, turn(): lax.dot_general(latent, grad_prod_b, (((0,), (0,)), ((), ())), preferred_...  39.4 us
    dot_general x5, matrix products, turn(): lax.dot_general(grad_latent, layer_in, (((0,), (0,)), ((), ())), preferre...  39.3 us
    all_to_all x1, waiting for transfers between devices, local(): lax.all_to_all(send_vals.astype(jnp.bfloat16), ('section', 'dp'), split_a...  24.9 us
    dot_general x5, matrix products, turn(): jnp.dot(latent, up_mat, preferred_element_type=jnp.float32) + bias_row  20.7 us
    dot_general x5, matrix products, turn(): lax.dot_general(layer_in, down_mat, (((1,), (1,)), ((), ())), preferred_e...  20.2 us
    scatter-add x1, other arithmetic, local(): jax.ops.segment_sum(got_vals.reshape(-1, E), got_rows.reshape(-1), num_se...  14.8 us
    broadcast_in_dim x1, other arithmetic, local(): stacked = jnp.concatenate([acc_down, acc_up, acc_bias[None]], axis=0)[None]  12 us
  transfers between devices with their start and end apart: 9, of which 8 were waited for; matrix products, arithmetic and copies ran while one was open for 47% of the time, Pallas kernels for 0%

commit v1 on v0

v1 whole, which is shorter than its diff:
```python
import functools

import jax
import jax.numpy as jnp
from jax import lax
from jax.experimental import pallas as pl
from jax.experimental.pallas import tpu as pltpu
from jax.sharding import PartitionSpec as P

E = 256
ROWS_DEV = 2048
NT = (((1,), (1,)), ((), ()))
TN = (((0,), (0,)), ((), ()))
LAG = 3


def relay_kernel(
    sections,
    micro_count,
    rows,
    emb,
    sav,
    cot,
    wd,
    wu,
    bias,
    prod_out,
    glat_out,
    lat_out,
    bias_out,
    home_out,
    gbuf,
    gsend,
    dbuf,
    dsend,
    ubuf,
    usend,
    term_ref,
    gs,
    gr,
    ds,
    dr,
    us,
    ur,
):
    s = lax.axis_index("section")
    chunks = sections * micro_count
    top = sections - 1
    barrier = pltpu.get_barrier_semaphore()

    def greet(step):
        pl.semaphore_signal(
            barrier, inc=1, device_id={"section": s + step}, device_id_type=pl.DeviceIdType.MESH
        )

    @pl.when(s > 0)
    def _():
        greet(-1)

    @pl.when(s < top)
    def _():
        greet(1)

    inner = (s > 0) & (s < top)

    @pl.when(inner)
    def _():
        pl.semaphore_wait(barrier, 2)

    @pl.when(jnp.logical_not(inner))
    def _():
        pl.semaphore_wait(barrier, 1)

    def copy(src, dst, send, recv, j, step):
        return pltpu.make_async_remote_copy(
            src_ref=src.at[j],
            dst_ref=dst.at[j],
            send_sem=send.at[j],
            recv_sem=recv.at[j],
            device_id={"section": s + step},
            device_id_type=pl.DeviceIdType.MESH,
        )

    def g_copy(j):
        return copy(gsend, gbuf, gs, gr, j, -1)

    def d_copy(j):
        return copy(dsend, dbuf, ds, dr, j, -1)

    def u_copy(j):
        return copy(usend, ubuf, us, ur, j, 1)

    bias_out[...] = jnp.zeros_like(bias_out)

    def main(j):
        q = top - j // micro_count
        m = j % micro_count
        at = pl.ds(pl.multiple_of(q * rows, rows), rows)

        @pl.when(s == top)
        def _():
            gbuf[j] = cot[m, at, :]

        @pl.when(s < top)
        def _():
            g_copy(j).wait_recv()

        g32 = gbuf[j].astype(jnp.float32)
        gp = g32 * emb[m, at, :].astype(jnp.float32)
        gpb = gp.astype(jnp.bfloat16)
        prod_out[m, at, :] = gpb
        bias_out[...] += jnp.sum(gp, axis=0, keepdims=True)
        glat = lax.dot_general(gpb, wu[...], NT, preferred_element_type=jnp.float32).astype(
            jnp.bfloat16
        )
        glat_out[m, at, :] = glat
        passed = gbuf[j].astype(jnp.float32) + jnp.dot(
            glat, wd[...], preferred_element_type=jnp.float32
        )

        @pl.when(s > 0)
        def _():
            gsend[j] = passed.astype(jnp.bfloat16)
            g_copy(j).start()
            term_ref[j] = jnp.zeros(term_ref.shape[1:], jnp.float32)

        @pl.when(s == 0)
        def _():
            term_ref[j] = passed

        lat = lax.dot_general(
            sav[m, at, :], wd[...], NT, preferred_element_type=jnp.float32
        ).astype(jnp.bfloat16)
        lat_out[m, at, :] = lat
        product = jnp.dot(lat, wu[...], preferred_element_type=jnp.float32) + bias[...]
        term_ref[j] += gbuf[j].astype(jnp.float32) * product

        @pl.when((s >= q) & (s < top))
        def _():
            d_copy(j).wait_recv()
            term_ref[j] += dbuf[j].astype(jnp.float32)

        @pl.when(s > q)
        def _():
            dsend[j] = term_ref[j].astype(jnp.bfloat16)
            d_copy(j).start()

    def upward(j):
        q = top - j // micro_count
        m = j % micro_count

        @pl.when((s > 0) & (s <= q))
        def _():
            u_copy(j).wait_recv()
            term_ref[j] += ubuf[j].astype(jnp.float32)

        @pl.when(s < q)
        def _():
            usend[j] = term_ref[j].astype(jnp.bfloat16)
            u_copy(j).start()

        @pl.when(s == q)
        def _():
            home_out[m] = term_ref[j].astype(jnp.bfloat16)

    def step(i, carry):
        @pl.when(i < chunks)
        def _():
            main(i)

        j = i - LAG * s

        @pl.when((j >= 0) & (j < chunks))
        def _():
            upward(j)

        return carry

    lax.fori_loop(0, chunks + LAG * top, step, 0)

    def finish(j, carry):
        q = top - j // micro_count

        @pl.when(s > 0)
        def _():
            g_copy(j).wait_send()

        @pl.when(s > q)
        def _():
            d_copy(j).wait_send()

        @pl.when(s < q)
        def _():
            u_copy(j).wait_send()

        return carry

    lax.fori_loop(0, chunks, finish, 0)


def relay(sections, embedded, saved, cotangent, down, up, bias):
    micro_count, samples, width = embedded.shape
    rank = down.shape[0]
    rows = samples // sections
    chunks = sections * micro_count
    b16, f32 = jnp.bfloat16, jnp.float32
    vm = pl.BlockSpec(memory_space=pltpu.VMEM)
    dma = pltpu.SemaphoreType.DMA((chunks,))
    block = pltpu.VMEM((chunks, rows, width), b16)
    return pl.pallas_call(
        functools.partial(relay_kernel, sections, micro_count, rows),
        out_shape=(
            jax.ShapeDtypeStruct((micro_count, samples, width), b16),
            jax.ShapeDtypeStruct((micro_count, samples, rank), b16),
            jax.ShapeDtypeStruct((micro_count, samples, rank), b16),
            jax.ShapeDtypeStruct((1, width), f32),
            jax.ShapeDtypeStruct((micro_count, rows, width), b16),
        ),
        in_specs=[vm] * 6,
        out_specs=(vm,) * 5,
        scratch_shapes=[block] * 6 + [pltpu.VMEM((chunks, rows, width), f32)] + [dma] * 6,
        compiler_params=pltpu.CompilerParams(
            collective_id=0, has_side_effects=True, vmem_limit_bytes=56 * 1024 * 1024
        ),
        cost_estimate=pl.CostEstimate(
            flops=8 * micro_count * samples * width * rank,
            bytes_accessed=300_000_000,
            transcendentals=0,
        ),
    )(embedded, saved, cotangent, down, up, bias)


def local(embedded, saved_inputs, cotangent, w_down, w_up, bias, owners, row_ids):
    sections = lax.axis_size("section")
    replicas = lax.axis_size("dp")
    section_id = lax.axis_index("section")
    micro_count, samples, width = embedded.shape
    b16, f32 = jnp.bfloat16, jnp.float32
    devices = sections * replicas
    sub_rows = samples // sections
    features = width // E

    def home(array):
        array = array.reshape(samples, micro_count, features)
        part = lax.dynamic_slice_in_dim(array, section_id * sub_rows, sub_rows, 0)
        return part.transpose(1, 0, 2).reshape(-1)

    own = home(owners)
    ids = home(row_ids)
    look = own.shape[0]
    capacity = max(2, (2 * look + devices - 1) // devices)
    targets = own[:, None] == jnp.arange(devices, dtype=jnp.int32)[None, :]
    order = jnp.arange(look, dtype=jnp.int32)
    before = (order[None, :] < order[:, None]).astype(b16)
    ranks = jnp.dot(before, targets.astype(b16), preferred_element_type=f32)
    rank_of = jnp.sum(jnp.where(targets, ranks, 0.0), axis=1).astype(jnp.int32)
    place = own * capacity + rank_of
    slots = jnp.arange(devices * capacity, dtype=jnp.int32)
    pick = (slots[:, None] == place[None, :]).astype(b16)
    digits = jnp.stack([ids // 64, ids % 64], axis=1).astype(b16)
    send_digits = jnp.dot(pick, digits, preferred_element_type=f32).astype(jnp.int32)
    send_rows = (send_digits[:, 0] * 64 + send_digits[:, 1]).reshape(devices, capacity)
    got_rows = lax.all_to_all(
        send_rows, ("section", "dp"), split_axis=0, concat_axis=0, tiled=True
    ).reshape(-1)

    prods, glat, lat, bias_part, home_grad = relay(
        sections, embedded, saved_inputs[0], cotangent, w_down[0], w_up[0], bias
    )

    flat = lambda array: array.reshape(-1, array.shape[-1])
    part_down = lax.dot_general(
        flat(glat), flat(saved_inputs[0]), TN, preferred_element_type=f32
    ).astype(b16)
    part_up = lax.dot_general(flat(lat), flat(prods), TN, preferred_element_type=f32).astype(b16)
    part = jnp.concatenate([part_down, part_up], axis=0)
    reduced = lax.psum_scatter(part, "dp", scatter_dimension=1, tiled=True).astype(f32)
    rank = w_down.shape[1]
    grad_down = reduced[None, :rank]
    grad_up = reduced[None, rank:]
    bias_all = lax.all_to_all(
        bias_part.reshape(replicas, -1), "dp", split_axis=0, concat_axis=0, tiled=True
    )
    grad_bias = jnp.sum(bias_all, axis=0)[None]

    row_grads = home_grad.reshape(-1, E)
    send_vals = jnp.dot(pick, row_grads, preferred_element_type=f32).astype(b16)
    got_vals = lax.all_to_all(
        send_vals.reshape(devices, capacity, E),
        ("section", "dp"),
        split_axis=0,
        concat_axis=0,
        tiled=True,
    ).reshape(-1, E)
    named = (jnp.arange(ROWS_DEV, dtype=jnp.int32)[:, None] == got_rows[None, :]).astype(b16)
    table_grad = jnp.dot(named, got_vals, preferred_element_type=f32)
    return (grad_down, grad_up, grad_bias, table_grad)


def solution(mesh):
    placed = (
        P(None, "dp", None),
        P("section", None, "dp", None),
        P(None, "dp", None),
        P("section", None, None),
        P("section", None, None),
        P("section", None),
        P("dp", None, None, None),
        P("dp", None, None),
    )
    return jax.shard_map(
        local,
        mesh=mesh,
        in_specs=placed,
        out_specs=(
            P("section", None, "dp"),
            P("section", None, "dp"),
            P("section", "dp"),
            P(("section", "dp"), None),
        ),
        check_vma=False,
    )
```

time: 364 us -> 225 us (0.62)
  matrix products: 136 us -> 17.4 us
  Pallas kernels: 0 us -> 112 us
  waiting for transfers between devices: 113 us -> 57.3 us
  other arithmetic: 52.8 us -> 10.7 us
  local copies, waits for them, and re-layouts: 27.4 us -> 3.49 us
  starting transfers between devices: 19.1 us -> 9.29 us
    dot_general x30 -> x6, matrix products: 136 us -> 17.4 us  [the longest x1 5.06 us: local(): lax.dot_general(flat(lat), flat(prods), TN, preferred_element_type=f32)]
    pallas_call x0 -> x1, Pallas kernels: none -> 112 us  [relay(): pl.pallas_call(functools.partial(relay_kernel, sections, micro_count, row...]
    reduce_scatter x2 -> x1, waiting for transfers between devices: 78.8 us -> 27.4 us  [local(): lax.psum_scatter(part, 'dp', scatter_dimension=1, tiled=True).astype(f32)]
    scatter-add x1 -> x0, other arithmetic: 14.8 us -> none  [local(): jax.ops.segment_sum(got_vals.reshape(-1, E), got_rows.reshape(-1), num_se...]
    broadcast_in_dim x1 -> x0, other arithmetic: 12 us -> none  [local(): stacked = jnp.concatenate([acc_down, acc_up, acc_bias[None]], axis=0)[None]]
    unnamed x15 -> x10, local copies, waits for them, and re-layouts: 10.8 us -> 0.03 us
    reduce_sum x6 -> x1, other arithmetic: 11.1 us -> 0.61 us  [local(): grad_bias = jnp.sum(bias_all, axis=0)[None]]
    ppermute x5 -> x0, waiting for transfers between devices: 9.22 us -> none  [from_behind(): return lax.ppermute(block, axis, route)]
  transfers between devices with their start and end apart: 9 -> 4, of which waited for: 8 -> 4; matrix products, arithmetic and copies ran while one was open for 47% -> 6% of each run, Pallas kernels for 0% -> 0%
where the time goes in v1:
time: 225 us; the launch traced here: 224 us
  Pallas kernels  112 us (50%)
  waiting for transfers between devices  57.3 us (25%)
  matrix products  17.4 us (8%)
  between operations  14.2 us (6%)
  other arithmetic  10.7 us (5%)
  starting transfers between devices  9.29 us (4%)
  local copies, waits for them, and re-layouts  3.49 us (2%)
    pallas_call x1, Pallas kernels, relay(): pl.pallas_call(functools.partial(relay_kernel, sections, micro_count, row...  112 us
    reduce_scatter x1, waiting for transfers between devices, local(): lax.psum_scatter(part, 'dp', scatter_dimension=1, tiled=True).astype(f32)  27.4 us
    all_to_all x1, waiting for transfers between devices, local(): lax.all_to_all(send_vals.reshape(devices, capacity, E), ('section', 'dp')...  24.1 us
    concatenate x1, other arithmetic, local(): part = jnp.concatenate([part_down, part_up], axis=0)  7.8 us
    dot_general x1, matrix products, local(): lax.dot_general(flat(lat), flat(prods), TN, preferred_element_type=f32)  5.06 us
    all_to_all x1, waiting for transfers between devices, local(): lax.all_to_all(send_rows, ('section', 'dp'), split_axis=0, concat_axis=0,...  4.5 us
  transfers between devices with their start and end apart: 4, of which 4 were waited for; matrix products, arithmetic and copies ran while one was open for 6% of the time, Pallas kernels for 0%

profile of v1, /device:TPU:0, one launch (start us, length us, event | category | flops | bytes accessed | tf_op | source)
XLA Modules:
  0.0 224.4 jit_solution(9759222247014345083)
XLA Ops:
  7.2 0.0 copy-start
  7.2 0.0 reduce-scatter.2.cloned.1.call-start
  7.2 112.1 %shard_map.111 = (bf16[2,128,4096]{2,1,0:T(8,128)(2,1)}, bf16[2,128,512]{2,1,0:T(8,128)(2,1)}, bf16[2,128,512]{2,1,0:T(8,128)(2,1)}, f32[1,4096]{1,0:T(1,128)}, bf16[2,32,4096]{2,1,0:T(8,128)(2,1)}) custom-call(bf16[2,128,4096]{2,1,0:T(8,128)(2,1)} %emb.1, bf16[2,128,4096]{2,1,0:T(8,128)(2,1)} %bitcast.30, bf16[2,128,4096]{2,1,0:T(8,128)(2,1)} %cot.1, ...), custom_call_target="tpu_custom_call" | custom-call | flops 4294967296 | bytes 300000000 | tf_op jit(solution)/shard_map/pallas_call | solution.py:210
  119.4 0.0 copy-start.1
  119.4 0.0 copy-start.3
  119.4 5.1 %bitcast_convert_fusion = bf16[512,4096]{1,0:T(8,128)(2,1)} fusion(bf16[2,128,512]{2,1,0:T(8,128)(2,1)} %get-tuple-element.10, bf16[2,128,4096]{2,1,0:T(8,128)(2,1)} %get-tuple-element.11), kind=kOutput, calls=%fused_computation.3 | convolution fusion | flops 1075838976 | bytes 6553600 | tf_op jit(solution)/shard_map/dot_general | solution.py:275
  124.4 0.0 copy-done.1
  124.4 0.0 copy-done.3
  124.4 3.2 %convolution_convert_fusion = bf16[512,4096]{1,0:T(8,128)(2,1)} fusion(bf16[256,512]{1,0:T(8,128)(2,1)S(1)} %bitcast.33, bf16[256,4096]{1,0:T(8,128)(2,1)S(1)} %bitcast.31), kind=kOutput, calls=%fused_computation.8 | convolution fusion | flops 1075838976 | bytes 6553600 | tf_op jit(solution)/shard_map/dot_general | solution.py:272
  127.7 7.8 %pad_maximum_fusion = bf16[1024,4096]{1,0:T(8,128)(2,1)} fusion(bf16[512,4096]{1,0:T(8,128)(2,1)} %bitcast_convert_fusion, bf16[512,4096]{1,0:T(8,128)(2,1)} %convolution_convert_fusion), kind=kLoop, calls=%fused_computation.2 | loop fusion | flops 16777216 | bytes 16777216 | tf_op jit(solution)/shard_map/concatenate | solution.py:276
  135.5 0.0 copy-start.4
  135.5 0.0 reduce-scatter.2.cloned.1.call-update
  135.5 0.0 copy-start.2
  135.5 3.9 %all-to-all-start = ((f32[8,1,512]{2,1,0:T(1,128)}), f32[8,1,512]{2,1,0:T(1,128)S(1)}, u32[]{:S(2)}, u32[]{:S(2)}) async-start(f32[8,1,512]{2,1,0:T(1,128)} %bitcast.8), calls=%async_computation.1 | async-start | bytes 32768 | tf_op jit(solution)/shard_map/all_to_all | solution.py:281
  139.4 0.0 copy-done
  139.4 0.1 dynamic-slice_bitcast_fusion.1
  139.5 0.1 copy.22
  139.5 0.1 reshape.177
  139.6 0.0 copy-done.4
  139.6 0.1 dynamic-slice_bitcast_fusion
  139.7 0.1 copy.23
  139.8 0.1 reshape.178
  139.9 0.5 fusion.10
  140.5 1.5 fusion.8
  142.0 0.0 copy-done.2
  142.0 0.2 reshape.179
  142.3 0.7 add.52
  142.9 1.2 all-to-all-done
  144.1 2.6 %all-to-all-start.1 = ((s32[32,1,64]{2,1,0:T(1,128)}), s32[32,1,64]{2,1,0:T(1,128)S(1)}, u32[]{:S(2)}, u32[]{:S(2)}) async-start(s32[32,1,64]{2,1,0:T(1,128)} %bitcast.14), calls=%async_computation.2 | async-start | bytes 32768 | tf_op jit(solution)/shard_map/all_to_all | solution.py:263
  146.7 2.6 %fusion.7 = bf16[2048,256]{1,0:T(8,128)(2,1)} fusion(bf16[1024,256]{1,0:T(8,128)(2,1)S(1)} %reshape.179, s32[1024]{0:T(1024)S(1)} %convert_add_fusion), kind=kOutput, calls=%fused_computation.13 | convolution fusion | flops 1076363264 | bytes 1576960 | tf_op jit(solution)/shard_map/dot_general | solution.py:287
  149.3 4.5 %all-to-all-done.1 = s32[32,1,64]{2,1,0:T(1,128)S(1)} async-done(((s32[32,1,64]{2,1,0:T(1,128)}), s32[32,1,64]{2,1,0:T(1,128)S(1)}, u32[]{:S(2)}, u32[]{:S(2)}) %all-to-all-start.1) | async-done | bytes 8224 | tf_op jit(solution)/shard_map/all_to_all | solution.py:263
  153.8 2.8 %all-to-all-start.2 = ((bf16[32,64,256]{2,1,0:T(8,128)(2,1)}), bf16[32,64,256]{2,1,0:T(8,128)(2,1)S(1)}, u32[]{:S(2)}, u32[]{:S(2)}) async-start(bf16[32,64,256]{2,1,0:T(8,128)(2,1)} %bitcast.15), calls=%async_computation.3 | async-start | bytes 2097152 | tf_op jit(solution)/shard_map/all_to_all | solution.py:288
  156.6 0.6 reduce_sum.18
  157.2 0.5 broadcast.111
  157.8 0.7 reduce.8
  158.5 0.1 eq.50
  158.5 24.1 %all-to-all-done.2 = bf16[32,64,256]{2,1,0:T(8,128)(2,1)S(1)} async-done(((bf16[32,64,256]{2,1,0:T(8,128)(2,1)}), bf16[32,64,256]{2,1,0:T(8,128)(2,1)S(1)}, u32[]{:S(2)}, u32[]{:S(2)}) %all-to-all-start.2) | async-done | bytes 1048608 | tf_op jit(solution)/shard_map/all_to_all | solution.py:288
  182.7 4.5 %fusion = f32[2048,256]{1,0:T(8,128)} fusion(bf16[2048,256]{1,0:T(8,128)(2,1)S(1)} %bitcast.32, s32[2048]{0:T(1024)S(1)} %eq.50), kind=kOutput, calls=%fused_computation.1 | convolution fusion | flops 2151677952 | bytes 3153920 | tf_op jit(solution)/shard_map/dot_general | solution.py:296
  187.1 27.4 %reduce-scatter.2.cloned.1.call-done = bf16[1024,512]{1,0:T(8,128)(2,1)} async-done(((bf16[1024,4096]{1,0:T(8,128)(2,1)}), bf16[1024,512]{1,0:T(8,128)(2,1)}) %reduce-scatter.2.cloned.1.call-update) | async-done | bytes 1048592 | tf_op jit(solution)/shard_map/reduce_scatter | solution.py:277
  214.6 1.5 convert_element_type.29
  216.1 1.5 slice_bitcast_fusion
  (4 shorter events, 0.1 us)
Async XLA Ops:
  7.2 132.2 %copy-start = (s32[128,2,16,1]{0,3,2,1:T(1,128)S(1)}, s32[128,2,16,1]{0,3,2,1:T(1,128)}, u32[]{:S(2)}) copy-start(s32[128,2,16,1]{0,3,2,1:T(1,128)} %param.14) | copy-start | bytes 49156
  7.2 207.4 %reduce-scatter.2.cloned.1.call-start = ((), (), s32[]{:S(2)}) async-start(), calls=%async_computation.4 | async-start | bytes 9437184 | tf_op jit(solution)/shard_map/reduce_scatter | solution.py:277
  119.4 5.1 %copy-start.1 = (bf16[1,2,128,4096]{3,2,1,0:T(8,128)(2,1)S(1)}, bf16[1,2,128,4096]{3,2,1,0:T(8,128)(2,1)}, u32[]{:S(2)}) copy-start(bf16[1,2,128,4096]{3,2,1,0:T(8,128)(2,1)} %param.9) | copy-start | bytes 6291460
  119.4 5.1 %copy-start.3 = (bf16[2,128,512]{2,1,0:T(8,128)(2,1)S(1)}, bf16[2,128,512]{2,1,0:T(8,128)(2,1)}, u32[]{:S(2)}) copy-start(bf16[2,128,512]{2,1,0:T(8,128)(2,1)} %get-tuple-element.9) | copy-start | bytes 786436
  135.5 4.1 %copy-start.4 = (s32[128,2,16]{0,2,1:T(8,128)S(1)}, s32[128,2,16]{0,2,1:T(8,128)}, u32[]{:S(2)}) copy-start(s32[128,2,16]{0,2,1:T(8,128)} %param.15) | copy-start | bytes 49156
  135.5 6.5 %copy-start.2 = (bf16[2,32,4096]{2,1,0:T(8,128)(2,1)S(1)}, bf16[2,32,4096]{2,1,0:T(8,128)(2,1)}, u32[]{:S(2)}) copy-start(bf16[2,32,4096]{2,1,0:T(8,128)(2,1)} %get-tuple-element.13) | copy-start | bytes 1572868
  135.5 8.6 %all-to-all-start = ((f32[8,1,512]{2,1,0:T(1,128)}), f32[8,1,512]{2,1,0:T(1,128)S(1)}, u32[]{:S(2)}, u32[]{:S(2)}) async-start(f32[8,1,512]{2,1,0:T(1,128)} %bitcast.8), calls=%async_computation.1 | async-start | bytes 32768 | tf_op jit(solution)/shard_map/all_to_all | solution.py:281
  144.1 9.7 %all-to-all-start.1 = ((s32[32,1,64]{2,1,0:T(1,128)}), s32[32,1,64]{2,1,0:T(1,128)S(1)}, u32[]{:S(2)}, u32[]{:S(2)}) async-start(s32[32,1,64]{2,1,0:T(1,128)} %bitcast.14), calls=%async_computation.2 | async-start | bytes 32768 | tf_op jit(solution)/shard_map/all_to_all | solution.py:263
  153.8 28.8 %all-to-all-start.2 = ((bf16[32,64,256]{2,1,0:T(8,128)(2,1)}), bf16[32,64,256]{2,1,0:T(8,128)(2,1)S(1)}, u32[]{:S(2)}, u32[]{:S(2)}) async-start(bf16[32,64,256]{2,1,0:T(8,128)(2,1)} %bitcast.15), calls=%async_computation.3 | async-start | bytes 2097152 | tf_op jit(solution)/shard_map/all_to_all | solution.py:288
Sparse Core Ops, SparseCore 0:
  135.6 78.8 reduce-scatter.1

commit v2 on v1

--- a/solution.py
+++ b/solution.py
@@ -16,6 +16,7 @@
 
 def relay_kernel(
     sections,
+    replicas,
     micro_count,
     rows,
     emb,
@@ -24,11 +25,15 @@
     wd,
     wu,
     bias,
-    prod_out,
-    glat_out,
-    lat_out,
+    down_out,
+    up_out,
     bias_out,
     home_out,
+    prod,
+    lg,
+    gall,
+    lall,
+    sall,
     gbuf,
     gsend,
     dbuf,
@@ -42,8 +47,17 @@
     dr,
     us,
     ur,
+    xs,
+    xr,
+    ls,
+    lr,
+    ss,
+    sr,
 ):
     s = lax.axis_index("section")
+    d = lax.axis_index("dp")
+    cols = gall.shape[-1]
+    rank = wd.shape[0]
     chunks = sections * micro_count
     top = sections - 1
     barrier = pltpu.get_barrier_semaphore()
@@ -61,15 +75,25 @@
     def _():
         greet(1)
 
+    def meet(k, carry):
+        pl.semaphore_signal(
+            barrier,
+            inc=1,
+            device_id={"dp": (d + k) % replicas},
+            device_id_type=pl.DeviceIdType.MESH,
+        )
+        return carry
+
+    lax.fori_loop(1, replicas, meet, 0)
     inner = (s > 0) & (s < top)
 
     @pl.when(inner)
     def _():
-        pl.semaphore_wait(barrier, 2)
+        pl.semaphore_wait(barrier, replicas + 1)
 
     @pl.when(jnp.logical_not(inner))
     def _():
-        pl.semaphore_wait(barrier, 1)
+        pl.semaphore_wait(barrier, replicas)
 
     def copy(src, dst, send, recv, j, step):
         return pltpu.make_async_remote_copy(
@@ -90,7 +114,55 @@
     def u_copy(j):
         return copy(usend, ubuf, us, ur, j, 1)
 
-    bias_out[...] = jnp.zeros_like(bias_out)
+    def spread(src, dst, send, recv, peer):
+        return pltpu.make_async_remote_copy(
+            src_ref=src,
+            dst_ref=dst,
+            send_sem=send,
+            recv_sem=recv,
+            device_id={"dp": peer},
+            device_id_type=pl.DeviceIdType.MESH,
+        )
+
+    def columns(who):
+        return pl.ds(pl.multiple_of(who * cols, cols), cols)
+
+    def block(who):
+        return pl.ds(who * micro_count, micro_count)
+
+    def rows_of(q):
+        return pl.ds(pl.multiple_of(q * rows, rows), rows)
+
+    def x_copy(k, q, slot):
+        peer = (d + k) % replicas
+        return spread(
+            prod.at[:, rows_of(q), columns(peer)],
+            gall.at[block(slot), rows_of(q), :],
+            xs.at[k, q],
+            xr.at[k, q],
+            peer,
+        )
+
+    def l_copy(k, q, slot):
+        return spread(
+            lg.at[:, rows_of(q), :],
+            lall.at[block(slot), rows_of(q), :],
+            ls.at[k, q],
+            lr.at[k, q],
+            (d + k) % replicas,
+        )
+
+    def s_copy(k, slot):
+        peer = (d + k) % replicas
+        return spread(
+            sav.at[:, :, columns(peer)], sall.at[block(slot)], ss.at[k], sr.at[k], peer
+        )
+
+    def send_saved(k, carry):
+        s_copy(k, d).start()
+        return carry
+
+    lax.fori_loop(1, replicas, send_saved, 0)
 
     def main(j):
         q = top - j // micro_count
@@ -108,12 +180,11 @@
         g32 = gbuf[j].astype(jnp.float32)
         gp = g32 * emb[m, at, :].astype(jnp.float32)
         gpb = gp.astype(jnp.bfloat16)
-        prod_out[m, at, :] = gpb
-        bias_out[...] += jnp.sum(gp, axis=0, keepdims=True)
+        prod[m, at, :] = gpb
         glat = lax.dot_general(gpb, wu[...], NT, preferred_element_type=jnp.float32).astype(
             jnp.bfloat16
         )
-        glat_out[m, at, :] = glat
+        lg[m, at, rank:] = glat
         passed = gbuf[j].astype(jnp.float32) + jnp.dot(
             glat, wd[...], preferred_element_type=jnp.float32
         )
@@ -131,7 +202,7 @@
         lat = lax.dot_general(
             sav[m, at, :], wd[...], NT, preferred_element_type=jnp.float32
         ).astype(jnp.bfloat16)
-        lat_out[m, at, :] = lat
+        lg[m, at, :rank] = lat
         product = jnp.dot(lat, wu[...], preferred_element_type=jnp.float32) + bias[...]
         term_ref[j] += gbuf[j].astype(jnp.float32) * product
 
@@ -144,6 +215,15 @@
         def _():
             dsend[j] = term_ref[j].astype(jnp.bfloat16)
             d_copy(j).start()
+
+        @pl.when(m == micro_count - 1)
+        def _():
+            def send(k, carry):
+                x_copy(k, q, d).start()
+                l_copy(k, q, d).start()
+                return carry
+
+            lax.fori_loop(1, replicas, send, 0)
 
     def upward(j):
         q = top - j // micro_count
@@ -197,8 +277,40 @@
 
     lax.fori_loop(0, chunks, finish, 0)
 
-
-def relay(sections, embedded, saved, cotangent, down, up, bias):
+    gall[block(d)] = prod[:, :, columns(d)]
+    lall[block(d)] = lg[...]
+    sall[block(d)] = sav[:, :, columns(d)]
+
+    def arrive(k, carry):
+        slot = (d - k + replicas) % replicas
+        s_copy(k, slot).wait_recv()
+        s_copy(k, d).wait_send()
+
+        def quarter(q, inner_carry):
+            x_copy(k, q, slot).wait_recv()
+            l_copy(k, q, slot).wait_recv()
+            x_copy(k, q, d).wait_send()
+            l_copy(k, q, d).wait_send()
+            return inner_carry
+
+        return lax.fori_loop(0, sections, quarter, carry)
+
+    lax.fori_loop(1, replicas, arrive, 0)
+    total = lall.shape[0] * lall.shape[1]
+    products = gall[...].reshape(total, cols)
+    bias_out[...] = jnp.sum(products.astype(jnp.float32), axis=0, keepdims=True)
+    up_out[...] = lax.dot_general(
+        lall[:, :, :rank].reshape(total, rank), products, TN, preferred_element_type=jnp.float32
+    )
+    down_out[...] = lax.dot_general(
+        lall[:, :, rank:].reshape(total, rank),
+        sall[...].reshape(total, cols),
+        TN,
+        preferred_element_type=jnp.float32,
+    )
+
+
+def relay(sections, replicas, embedded, saved, cotangent, down, up, bias):
     micro_count, samples, width = embedded.shape
     rank = down.shape[0]
     rows = samples // sections
@@ -207,18 +319,31 @@
     vm = pl.BlockSpec(memory_space=pltpu.VMEM)
     dma = pltpu.SemaphoreType.DMA((chunks,))
     block = pltpu.VMEM((chunks, rows, width), b16)
+    cols = width // replicas
+    held = replicas * micro_count
+    quarters = pltpu.SemaphoreType.DMA((replicas, sections))
     return pl.pallas_call(
-        functools.partial(relay_kernel, sections, micro_count, rows),
+        functools.partial(relay_kernel, sections, replicas, micro_count, rows),
         out_shape=(
-            jax.ShapeDtypeStruct((micro_count, samples, width), b16),
-            jax.ShapeDtypeStruct((micro_count, samples, rank), b16),
-            jax.ShapeDtypeStruct((micro_count, samples, rank), b16),
-            jax.ShapeDtypeStruct((1, width), f32),
+            jax.ShapeDtypeStruct((rank, cols), f32),
+            jax.ShapeDtypeStruct((rank, cols), f32),
+            jax.ShapeDtypeStruct((1, cols), f32),
             jax.ShapeDtypeStruct((micro_count, rows, width), b16),
         ),
         in_specs=[vm] * 6,
-        out_specs=(vm,) * 5,
-        scratch_shapes=[block] * 6 + [pltpu.VMEM((chunks, rows, width), f32)] + [dma] * 6,
+        out_specs=(vm,) * 4,
+        scratch_shapes=[
+            pltpu.VMEM((micro_count, samples, width), b16),
+            pltpu.VMEM((micro_count, samples, 2 * rank), b16),
+            pltpu.VMEM((held, samples, cols), b16),
+            pltpu.VMEM((held, samples, 2 * rank), b16),
+            pltpu.VMEM((held, samples, cols), b16),
+        ]
+        + [block] * 6
+        + [pltpu.VMEM((chunks, rows, width), f32)]
+        + [dma] * 6
+        + [quarters] * 4
+        + [pltpu.SemaphoreType.DMA((replicas,))] * 2,
         compiler_params=pltpu.CompilerParams(
             collective_id=0, has_side_effects=True, vmem_limit_bytes=56 * 1024 * 1024
         ),
@@ -264,24 +389,9 @@
         send_rows, ("section", "dp"), split_axis=0, concat_axis=0, tiled=True
     ).reshape(-1)
 
-    prods, glat, lat, bias_part, home_grad = relay(
-        sections, embedded, saved_inputs[0], cotangent, w_down[0], w_up[0], bias
+    grad_down, grad_up, grad_bias, home_grad = relay(
+        sections, replicas, embedded, saved_inputs[0], cotangent, w_down[0], w_up[0], bias
     )
-
-    flat = lambda array: array.reshape(-1, array.shape[-1])
-    part_down = lax.dot_general(
-        flat(glat), flat(saved_inputs[0]), TN, preferred_element_type=f32
-    ).astype(b16)
-    part_up = lax.dot_general(flat(lat), flat(prods), TN, preferred_element_type=f32).astype(b16)
-    part = jnp.concatenate([part_down, part_up], axis=0)
-    reduced = lax.psum_scatter(part, "dp", scatter_dimension=1, tiled=True).astype(f32)
-    rank = w_down.shape[1]
-    grad_down = reduced[None, :rank]
-    grad_up = reduced[None, rank:]
-    bias_all = lax.all_to_all(
-        bias_part.reshape(replicas, -1), "dp", split_axis=0, concat_axis=0, tiled=True
-    )
-    grad_bias = jnp.sum(bias_all, axis=0)[None]
 
     row_grads = home_grad.reshape(-1, E)
     send_vals = jnp.dot(pick, row_grads, preferred_element_type=f32).astype(b16)
@@ -294,7 +404,7 @@
     ).reshape(-1, E)
     named = (jnp.arange(ROWS_DEV, dtype=jnp.int32)[:, None] == got_rows[None, :]).astype(b16)
     table_grad = jnp.dot(named, got_vals, preferred_element_type=f32)
-    return (grad_down, grad_up, grad_bias, table_grad)
+    return (grad_down[None], grad_up[None], grad_bias, table_grad)
 
 
 def solution(mesh):

time: 225 us -> 183 us (0.81)
  waiting for transfers between devices: 57.3 us -> 24.7 us
  Pallas kernels: 112 us -> 129 us
  between operations: 14.2 us -> 0.73 us
  other arithmetic: 10.7 us -> 0.77 us
  matrix products: 17.4 us -> 9.08 us
  local copies, waits for them, and re-layouts: 3.49 us -> 6.96 us
    reduce_scatter x1 -> x0, waiting for transfers between devices: 27.4 us -> none  [local(): lax.psum_scatter(part, 'dp', scatter_dimension=1, tiled=True).astype(f32)]
    pallas_call x1, Pallas kernels: 112 us -> 129 us  [relay(): pl.pallas_call(functools.partial(relay_kernel, sections, replicas, micro_...]
    dot_general x2 -> x0, matrix products: 8.28 us -> none  [the longest x1 5.06 us: local(): lax.dot_general(flat(lat), flat(prods), TN, preferred_element_type=f32)]
    concatenate x1 -> x0, other arithmetic: 7.8 us -> none  [local(): part = jnp.concatenate([part_down, part_up], axis=0)]
    all_to_all x1, starting transfers between devices: 2.56 us -> 7.33 us  [local(): lax.all_to_all(send_rows, ('section', 'dp'), split_axis=0, concat_axis=0,...]
    all_to_all x1, waiting for transfers between devices: 4.5 us -> 0.01 us  [local(): lax.all_to_all(send_rows, ('section', 'dp'), split_axis=0, concat_axis=0,...]
    all_to_all x1 -> x0, starting transfers between devices: 3.86 us -> none  [local(): lax.all_to_all(bias_part.reshape(replicas, -1), 'dp', split_axis=0, conca...]
    unnamed x10 -> x11, local copies, waits for them, and re-layouts: 0.03 us -> 3.24 us
  transfers between devices with their start and end apart: 4 -> 2, of which waited for: 4 -> 1; matrix products, arithmetic and copies ran while one was open for 6% -> 3% of each run, Pallas kernels for 0% -> 71%
where the time goes in v2:
time: 183 us; the launch traced here: 182 us
  Pallas kernels  129 us (70%)
  waiting for transfers between devices  24.7 us (13%)
  starting transfers between devices  10.6 us (6%)
  matrix products  9.08 us (5%)
  local copies, waits for them, and re-layouts  6.96 us (4%)
    pallas_call x1, Pallas kernels, relay(): pl.pallas_call(functools.partial(relay_kernel, sections, replicas, micro_...  129 us
    all_to_all x1, waiting for transfers between devices, local(): lax.all_to_all(send_vals.reshape(devices, capacity, E), ('section', 'dp')...  24.7 us
    all_to_all x1, starting transfers between devices, local(): lax.all_to_all(send_rows, ('section', 'dp'), split_axis=0, concat_axis=0,...  7.33 us
    dot_general x1, matrix products, local(): table_grad = jnp.dot(named, got_vals, preferred_element_type=f32)  4.46 us
  transfers between devices with their start and end apart: 2, of which 1 were waited for; matrix products, arithmetic and copies ran while one was open for 3% of the time, Pallas kernels for 71%

profile of v2, /device:TPU:0, one launch (start us, length us, event | category | flops | bytes accessed | tf_op | source)
XLA Modules:
  0.0 182.3 jit_solution(9880486140199471438)
XLA Ops:
  0.6 0.0 copy-start
  0.7 0.7 copy-done
  1.4 0.1 dynamic-slice_bitcast_fusion.1
  1.4 0.8 dynamic-slice_bitcast_fusion
  2.2 0.1 copy.18
  2.3 0.1 reshape.168
  2.4 0.1 copy.17
  2.5 0.1 reshape.167
  2.6 0.5 fusion.10
  3.1 1.5 fusion.8
  4.7 0.7 add.50
  5.3 7.3 %all-to-all-start = ((s32[32,1,64]{2,1,0:T(1,128)}), s32[32,1,64]{2,1,0:T(1,128)S(1)}, u32[]{:S(2)}, u32[]{:S(2)}) async-start(s32[32,1,64]{2,1,0:T(1,128)} %bitcast.9), calls=%async_computation | async-start | bytes 32768 | tf_op jit(solution)/shard_map/all_to_all | solution.py:388
  12.7 129.4 %shard_map.111 = (f32[512,512]{1,0:T(8,128)}, f32[512,512]{1,0:T(8,128)}, f32[1,512]{1,0:T(1,128)}, bf16[2,32,4096]{2,1,0:T(8,128)(2,1)}) custom-call(bf16[2,128,4096]{2,1,0:T(8,128)(2,1)} %emb.1, bf16[2,128,4096]{2,1,0:T(8,128)(2,1)} %bitcast.23, bf16[2,128,4096]{2,1,0:T(8,128)(2,1)} %cot.1, bf16[512,4096]{1,0:T(8,128)(2,1)} %bitcast.21, ...), custom_call_target="tpu_custom_call" | custom-call | flops 4294967296 | bytes 300000000 | tf_op jit(solution)/shard_map/pallas_call | solution.py:325
  142.1 1.3 reshape.169
  143.4 2.6 %fusion.7 = bf16[2048,256]{1,0:T(8,128)(2,1)} fusion(bf16[1024,256]{1,0:T(8,128)(2,1)S(1)} %reshape.169, s32[1024]{0:T(1024)S(1)} %convert_add_fusion), kind=kOutput, calls=%fused_computation.10 | convolution fusion | flops 1076363264 | bytes 1576960 | tf_op jit(solution)/shard_map/dot_general | solution.py:397
  146.0 0.0 all-to-all-done
  146.0 3.3 %all-to-all-start.1 = ((bf16[32,64,256]{2,1,0:T(8,128)(2,1)}), bf16[32,64,256]{2,1,0:T(8,128)(2,1)S(1)}, u32[]{:S(2)}, u32[]{:S(2)}) async-start(bf16[32,64,256]{2,1,0:T(8,128)(2,1)} %bitcast.10), calls=%async_computation.1 | async-start | bytes 2097152 | tf_op jit(solution)/shard_map/all_to_all | solution.py:398
  149.2 0.5 broadcast.111
  149.7 0.7 reduce.7
  150.4 0.1 eq.50
  150.5 24.7 %all-to-all-done.1 = bf16[32,64,256]{2,1,0:T(8,128)(2,1)S(1)} async-done(((bf16[32,64,256]{2,1,0:T(8,128)(2,1)}), bf16[32,64,256]{2,1,0:T(8,128)(2,1)S(1)}, u32[]{:S(2)}, u32[]{:S(2)}) %all-to-all-start.1) | async-done | bytes 1048608 | tf_op jit(solution)/shard_map/all_to_all | solution.py:398
  175.3 0.0 copy-start.2
  175.3 0.0 copy-start.1
  175.3 4.5 %fusion = f32[2048,256]{1,0:T(8,128)} fusion(bf16[2048,256]{1,0:T(8,128)(2,1)S(1)} %bitcast.20, s32[2048]{0:T(1024)S(1)} %eq.50), kind=kOutput, calls=%fused_computation.1 | convolution fusion | flops 2151677952 | bytes 3153920 | tf_op jit(solution)/shard_map/dot_general | solution.py:406
  179.7 0.0 copy-done.2
  179.7 0.0 copy-start.3
  179.7 1.0 copy.23
  180.7 0.0 copy-done.1
  180.7 1.0 copy.24
  181.7 0.0 copy-done.3
  181.7 0.6 copy.25
  (4 shorter events, 0.1 us)
Async XLA Ops:
  0.6 0.7 copy-start
  5.3 140.6 %all-to-all-start = ((s32[32,1,64]{2,1,0:T(1,128)}), s32[32,1,64]{2,1,0:T(1,128)S(1)}, u32[]{:S(2)}, u32[]{:S(2)}) async-start(s32[32,1,64]{2,1,0:T(1,128)} %bitcast.9), calls=%async_computation | async-start | bytes 32768 | tf_op jit(solution)/shard_map/all_to_all | solution.py:388
  146.0 29.3 %all-to-all-start.1 = ((bf16[32,64,256]{2,1,0:T(8,128)(2,1)}), bf16[32,64,256]{2,1,0:T(8,128)(2,1)S(1)}, u32[]{:S(2)}, u32[]{:S(2)}) async-start(bf16[32,64,256]{2,1,0:T(8,128)(2,1)} %bitcast.10), calls=%async_computation.1 | async-start | bytes 2097152 | tf_op jit(solution)/shard_map/all_to_all | solution.py:398
  175.3 4.5 %copy-start.2 = (f32[512,512]{1,0:T(8,128)S(1)}, f32[512,512]{1,0:T(8,128)}, u32[]{:S(2)}) copy-start(f32[512,512]{1,0:T(8,128)} %get-tuple-element.8) | copy-start | bytes 3145732
  175.3 5.4 %copy-start.1 = (f32[512,512]{1,0:T(8,128)S(1)}, f32[512,512]{1,0:T(8,128)}, u32[]{:S(2)}) copy-start(f32[512,512]{1,0:T(8,128)} %get-tuple-element.9) | copy-start | bytes 3145732
  179.7 1.9 %copy-start.3 = (f32[1,512]{1,0:T(1,128)S(1)}, f32[1,512]{1,0:T(1,128)}, u32[]{:S(2)}) copy-start(f32[1,512]{1,0:T(1,128)} %get-tuple-element.20) | copy-start | bytes 6148

commit v3 on v2

--- a/solution.py
+++ b/solution.py
@@ -12,6 +12,7 @@
 NT = (((1,), (1,)), ((), ()))
 TN = (((0,), (0,)), ((), ()))
 LAG = 3
+DOWN_LAG = 3
 
 
 def relay_kernel(
@@ -206,16 +207,6 @@
         product = jnp.dot(lat, wu[...], preferred_element_type=jnp.float32) + bias[...]
         term_ref[j] += gbuf[j].astype(jnp.float32) * product
 
-        @pl.when((s >= q) & (s < top))
-        def _():
-            d_copy(j).wait_recv()
-            term_ref[j] += dbuf[j].astype(jnp.float32)
-
-        @pl.when(s > q)
-        def _():
-            dsend[j] = term_ref[j].astype(jnp.bfloat16)
-            d_copy(j).start()
-
         @pl.when(m == micro_count - 1)
         def _():
             def send(k, carry):
@@ -225,9 +216,21 @@
 
             lax.fori_loop(1, replicas, send, 0)
 
+    def downward(j):
+        q = top - j // micro_count
+
+        @pl.when((s >= q) & (s < top))
+        def _():
+            d_copy(j).wait_recv()
+            term_ref[j] += dbuf[j].astype(jnp.float32)
+
+        @pl.when(s > q)
+        def _():
+            dsend[j] = term_ref[j].astype(jnp.bfloat16)
+            d_copy(j).start()
+
     def upward(j):
         q = top - j // micro_count
-        m = j % micro_count
 
         @pl.when((s > 0) & (s <= q))
         def _():
@@ -239,15 +242,17 @@
             usend[j] = term_ref[j].astype(jnp.bfloat16)
             u_copy(j).start()
 
-        @pl.when(s == q)
-        def _():
-            home_out[m] = term_ref[j].astype(jnp.bfloat16)
-
     def step(i, carry):
         @pl.when(i < chunks)
         def _():
             main(i)
 
+        behind = i - DOWN_LAG
+
+        @pl.when((behind >= 0) & (behind < chunks))
+        def _():
+            downward(behind)
+
         j = i - LAG * s
 
         @pl.when((j >= 0) & (j < chunks))
@@ -256,7 +261,9 @@
 
         return carry
 
-    lax.fori_loop(0, chunks + LAG * top, step, 0)
+    lax.fori_loop(0, chunks + max(LAG * top, DOWN_LAG), step, 0)
+    for m in range(micro_count):
+        home_out[m] = term_ref[(top - s) * micro_count + m].astype(jnp.bfloat16)
 
     def finish(j, carry):
         q = top - j // micro_count

time: 183 us -> 171 us (0.934)
  Pallas kernels: 129 us -> 117 us
    pallas_call x1, Pallas kernels: 129 us -> 117 us  [relay(): pl.pallas_call(functools.partial(relay_kernel, sections, replicas, micro_...]
  transfers between devices with their start and end apart: 2 -> 2, of which waited for: 1 -> 1; matrix products, arithmetic and copies ran while one was open for 3% -> 3% of each run, Pallas kernels for 71% -> 69%
where the time goes in v3:
time: 171 us; the launch traced here: 170 us
  Pallas kernels  117 us (68%)
  waiting for transfers between devices  24.7 us (14%)
  starting transfers between devices  10.7 us (6%)
  matrix products  9.07 us (5%)
  local copies, waits for them, and re-layouts  6.96 us (4%)
    pallas_call x1, Pallas kernels, relay(): pl.pallas_call(functools.partial(relay_kernel, sections, replicas, micro_...  117 us
    all_to_all x1, waiting for transfers between devices, local(): lax.all_to_all(send_vals.reshape(devices, capacity, E), ('section', 'dp')...  24.7 us
    all_to_all x1, starting transfers between devices, local(): lax.all_to_all(send_rows, ('section', 'dp'), split_axis=0, concat_axis=0,...  7.33 us
    dot_general x1, matrix products, local(): table_grad = jnp.dot(named, got_vals, preferred_element_type=f32)  4.46 us
  transfers between devices with their start and end apart: 2, of which 1 were waited for; matrix products, arithmetic and copies ran while one was open for 3% of the time, Pallas kernels for 69%

profile of v3, /device:TPU:0, one launch (start us, length us, event | category | flops | bytes accessed | tf_op | source)
XLA Modules:
  0.0 170.1 jit_solution(15210696923677719570)
XLA Ops:
  0.6 0.0 copy-start
  0.7 0.7 copy-done
  1.4 0.1 dynamic-slice_bitcast_fusion.1
  1.4 0.8 dynamic-slice_bitcast_fusion
  2.2 0.1 copy.18
  2.3 0.1 reshape.168
  2.4 0.1 copy.17
  2.5 0.1 reshape.167
  2.6 0.5 fusion.10
  3.1 1.5 fusion.8
  4.7 0.7 add.50
  5.3 7.3 %all-to-all-start = ((s32[32,1,64]{2,1,0:T(1,128)}), s32[32,1,64]{2,1,0:T(1,128)S(1)}, u32[]{:S(2)}, u32[]{:S(2)}) async-start(s32[32,1,64]{2,1,0:T(1,128)} %bitcast.9), calls=%async_computation | async-start | bytes 32768 | tf_op jit(solution)/shard_map/all_to_all | solution.py:395
  12.7 117.1 %shard_map.111 = (f32[512,512]{1,0:T(8,128)}, f32[512,512]{1,0:T(8,128)}, f32[1,512]{1,0:T(1,128)}, bf16[2,32,4096]{2,1,0:T(8,128)(2,1)}) custom-call(bf16[2,128,4096]{2,1,0:T(8,128)(2,1)} %emb.1, bf16[2,128,4096]{2,1,0:T(8,128)(2,1)} %bitcast.23, bf16[2,128,4096]{2,1,0:T(8,128)(2,1)} %cot.1, bf16[512,4096]{1,0:T(8,128)(2,1)} %bitcast.21, ...), custom_call_target="tpu_custom_call" | custom-call | flops 4294967296 | bytes 300000000 | tf_op jit(solution)/shard_map/pallas_call | solution.py:332
  129.8 1.3 reshape.169
  131.1 2.6 %fusion.7 = bf16[2048,256]{1,0:T(8,128)(2,1)} fusion(bf16[1024,256]{1,0:T(8,128)(2,1)S(1)} %reshape.169, s32[1024]{0:T(1024)S(1)} %convert_add_fusion), kind=kOutput, calls=%fused_computation.10 | convolution fusion | flops 1076363264 | bytes 1576960 | tf_op jit(solution)/shard_map/dot_general | solution.py:404
  133.7 0.0 all-to-all-done
  133.7 3.4 %all-to-all-start.1 = ((bf16[32,64,256]{2,1,0:T(8,128)(2,1)}), bf16[32,64,256]{2,1,0:T(8,128)(2,1)S(1)}, u32[]{:S(2)}, u32[]{:S(2)}) async-start(bf16[32,64,256]{2,1,0:T(8,128)(2,1)} %bitcast.10), calls=%async_computation.1 | async-start | bytes 2097152 | tf_op jit(solution)/shard_map/all_to_all | solution.py:405
  137.1 0.5 broadcast.111
  137.6 0.7 reduce.7
  138.3 0.1 eq.50
  138.4 24.7 %all-to-all-done.1 = bf16[32,64,256]{2,1,0:T(8,128)(2,1)S(1)} async-done(((bf16[32,64,256]{2,1,0:T(8,128)(2,1)}), bf16[32,64,256]{2,1,0:T(8,128)(2,1)S(1)}, u32[]{:S(2)}, u32[]{:S(2)}) %all-to-all-start.1) | async-done | bytes 1048608 | tf_op jit(solution)/shard_map/all_to_all | solution.py:405
  163.1 0.0 copy-start.2
  163.1 0.0 copy-start.1
  163.1 4.5 %fusion = f32[2048,256]{1,0:T(8,128)} fusion(bf16[2048,256]{1,0:T(8,128)(2,1)S(1)} %bitcast.20, s32[2048]{0:T(1024)S(1)} %eq.50), kind=kOutput, calls=%fused_computation.1 | convolution fusion | flops 2151677952 | bytes 3153920 | tf_op jit(solution)/shard_map/dot_general | solution.py:413
  167.6 0.0 copy-done.2
  167.6 0.0 copy-start.3
  167.6 1.0 copy.23
  168.6 0.0 copy-done.1
  168.6 1.0 copy.24
  169.5 0.0 copy-done.3
  169.5 0.6 copy.25
  (4 shorter events, 0.1 us)
Async XLA Ops:
  0.6 0.7 copy-start
  5.3 128.4 %all-to-all-start = ((s32[32,1,64]{2,1,0:T(1,128)}), s32[32,1,64]{2,1,0:T(1,128)S(1)}, u32[]{:S(2)}, u32[]{:S(2)}) async-start(s32[32,1,64]{2,1,0:T(1,128)} %bitcast.9), calls=%async_computation | async-start | bytes 32768 | tf_op jit(solution)/shard_map/all_to_all | solution.py:395
  133.7 29.4 %all-to-all-start.1 = ((bf16[32,64,256]{2,1,0:T(8,128)(2,1)}), bf16[32,64,256]{2,1,0:T(8,128)(2,1)S(1)}, u32[]{:S(2)}, u32[]{:S(2)}) async-start(bf16[32,64,256]{2,1,0:T(8,128)(2,1)} %bitcast.10), calls=%async_computation.1 | async-start | bytes 2097152 | tf_op jit(solution)/shard_map/all_to_all | solution.py:405
  163.1 4.5 %copy-start.2 = (f32[512,512]{1,0:T(8,128)S(1)}, f32[512,512]{1,0:T(8,128)}, u32[]{:S(2)}) copy-start(f32[512,512]{1,0:T(8,128)} %get-tuple-element.8) | copy-start | bytes 3145732
  163.1 5.4 %copy-start.1 = (f32[512,512]{1,0:T(8,128)S(1)}, f32[512,512]{1,0:T(8,128)}, u32[]{:S(2)}) copy-start(f32[512,512]{1,0:T(8,128)} %get-tuple-element.9) | copy-start | bytes 3145732
  167.6 1.9 %copy-start.3 = (f32[1,512]{1,0:T(1,128)S(1)}, f32[1,512]{1,0:T(1,128)}, u32[]{:S(2)}) copy-start(f32[1,512]{1,0:T(1,128)} %get-tuple-element.20) | copy-start | bytes 6148
